TPU v7x, 32 devices: a whole 2x2x4 slice. The times are simulated.
32 devices in a mesh: groups: 2 (over y), ulysses: 8 (over z, x), seq: 2 (over core).
Axes of the slice: x: 2, y: 2, z: 4, core: 2. Of those that a mesh axis runs over, the one named last changes fastest.
Arguments:
- query_states: bfloat16 [2048, 8192], P(('groups', 'ulysses', 'seq')), parts along dimension 0, may hold values from -6 to 6
- key_states: bfloat16 [2048, 1024], P(('groups', 'ulysses', 'seq')), parts along dimension 0, may hold values from -6 to 6
- value_states: bfloat16 [2048, 1024], P(('groups', 'ulysses', 'seq')), parts along dimension 0, may hold values from -6 to 6
- turn_ids: int32 [2048], P('groups'), parts along dimension 0, may hold values from 0 to 3, never falling along the last dimension, each value on 1 to 512 neighbouring positions
- judge_positions: int32 [256], P('groups'), parts along dimension 0, may hold values from 0 to 1023, as said below
Outputs:
- attended_states: bfloat16 [2048, 8192], P(('groups', 'ulysses', 'seq')), parts along dimension 0
There are 2 independent parts, one for each index of `groups`. A program takes and returns all parts, laid end to end along the dimension named above; each array names one. Nothing has to cross between parts.
Inputs may be any that keep to these rules, and one draw needn't show every extreme that they name: `turn_ids`: turn numbers never fall along the conversation; every turn spans 1 to 512 tokens, one exactly that many. `judge_positions`: distinct positions, 0 and 1023 among them.
All inputs are finite; a program needn't handle non-finite values.
Results may differ from a plain program's by a relative error of at most 0.004.
Values may be sent and summed in bfloat16 or wider, within the bound.
No kernel may reach another device: no remote copies, remote signals or barrier semaphores. Data moves between devices by JAX's collectives and lax.ppermute only.
A program may use at most 64 MiB of HBM per device.

v0:
```python
import math
import jax
import jax.numpy as jnp
from jax import lax
from jax.sharding import PartitionSpec as P

HEAD_DIM = 128
floor_score = -1e30


def absorb(
    carried,
    query_block,
    query_place,
    query_turn,
    keys_block,
    values_block,
    keys_place,
    keys_turn,
    keys_judge,
    scaling,
):
    maxima, totals, running = carried
    scores = (
        jnp.einsum("qhd,kd->qhk", query_block, keys_block, preferred_element_type=jnp.float32)
        * scaling
    )
    visible = (keys_place[None, :] <= query_place[:, None]) & (
        (keys_turn[None, :] == query_turn[:, None]) | keys_judge[None, :]
    )
    scores = jnp.where(visible[:, None, :], scores, floor_score)
    newest = jnp.maximum(maxima, jnp.max(scores, axis=2))
    factor = jnp.exp(maxima - newest)
    weights = jnp.exp(scores - newest[:, :, None])
    totals = totals * factor + jnp.sum(weights, axis=2)
    running = running * factor[:, :, None] + jnp.einsum(
        "qhk,kd->qhd",
        weights.astype(jnp.bfloat16),
        values_block,
        preferred_element_type=jnp.float32,
    )
    return (newest, totals, running)


def attend(
    carried,
    queries,
    query_place,
    query_turn,
    key_rows,
    value_rows,
    keys_place,
    keys_turn,
    keys_judge,
    scaling,
):
    query_count = queries.shape[0]
    key_count = key_rows.shape[0]
    query_step = math.gcd(query_count, 512)
    key_step = math.gcd(key_count, 512)

    def over_queries(row_index, totals_all):
        offset = row_index * query_step
        query_block = lax.dynamic_slice_in_dim(queries, offset, query_step, 0)
        block_place = lax.dynamic_slice_in_dim(query_place, offset, query_step, 0)
        block_turn = lax.dynamic_slice_in_dim(query_turn, offset, query_step, 0)
        window = tuple(
            (lax.dynamic_slice_in_dim(member, offset, query_step, 0) for member in totals_all)
        )

        def over_keys(key_index, current):
            key_offset = key_index * key_step
            keys_block = lax.dynamic_slice_in_dim(key_rows, key_offset, key_step, 0)
            values_block = lax.dynamic_slice_in_dim(value_rows, key_offset, key_step, 0)
            block_keys_place = lax.dynamic_slice_in_dim(keys_place, key_offset, key_step, 0)
            block_keys_turn = lax.dynamic_slice_in_dim(keys_turn, key_offset, key_step, 0)
            block_keys_judge = lax.dynamic_slice_in_dim(keys_judge, key_offset, key_step, 0)
            return lax.cond(
                jnp.max(block_place) >= jnp.min(block_keys_place),
                lambda inside: absorb(
                    inside,
                    query_block,
                    block_place,
                    block_turn,
                    keys_block,
                    values_block,
                    block_keys_place,
                    block_keys_turn,
                    block_keys_judge,
                    scaling,
                ),
                lambda inside: inside,
                current,
            )

        window = lax.fori_loop(0, key_count // key_step, over_keys, window)
        return tuple(
            (
                lax.dynamic_update_slice_in_dim(member, updated, offset, 0)
                for member, updated in zip(totals_all, window)
            )
        )

    return lax.fori_loop(0, query_count // query_step, over_queries, carried)


def spread(array, copies):
    row_count = array.shape[0]
    shared_heads = array.shape[1] // HEAD_DIM
    widened = jnp.broadcast_to(
        array.reshape(row_count, shared_heads, 1, HEAD_DIM),
        (row_count, shared_heads, copies // shared_heads, HEAD_DIM),
    )
    return widened.reshape(row_count, copies, HEAD_DIM)


def shards(query_states, key_states, value_states, turn_ids, judge_positions):
    tokens_here = query_states.shape[0]
    ulysses_count = lax.axis_size("ulysses")
    stripe_count = lax.axis_size("seq")
    stripe = lax.axis_index("seq")
    heads_here = query_states.shape[1] // HEAD_DIM // ulysses_count
    seq_total = tokens_here * ulysses_count * stripe_count
    scaling = 1.0 / math.sqrt(HEAD_DIM)
    positions = jnp.arange(seq_total, dtype=jnp.int32)
    judged = jnp.any(positions[:, None] == judge_positions[None, :], axis=1)
    exchanged = lax.all_to_all(
        query_states.reshape(tokens_here, ulysses_count, heads_here * HEAD_DIM),
        "ulysses",
        split_axis=1,
        concat_axis=0,
        tiled=True,
    )
    query_total = ulysses_count * tokens_here
    queries = exchanged.reshape(query_total, heads_here, HEAD_DIM)
    local_rows = jnp.arange(query_total, dtype=jnp.int32)
    query_place = (
        local_rows // tokens_here * stripe_count + stripe
    ) * tokens_here + local_rows % tokens_here
    query_turn = jnp.take(turn_ids, query_place)
    carried = (
        jnp.full((query_total, heads_here), floor_score, jnp.float32),
        jnp.zeros((query_total, heads_here), jnp.float32),
        jnp.zeros((query_total, heads_here, HEAD_DIM), jnp.float32),
    )
    keys_out, values_out = (
        lax.all_to_all(
            spread(key_states, ulysses_count), "ulysses", split_axis=1, concat_axis=0, tiled=True
        ),
        lax.all_to_all(
            spread(value_states, ulysses_count), "ulysses", split_axis=1, concat_axis=0, tiled=True
        ),
    )
    key_rows = keys_out.reshape(query_total, HEAD_DIM)
    value_rows = values_out.reshape(query_total, HEAD_DIM)
    pieces = (
        lax.all_gather(key_rows, "seq", axis=0, tiled=True),
        lax.all_gather(value_rows, "seq", axis=0, tiled=True),
    )
    piece_rows = pieces[0].shape[0]
    gathered_rows = jnp.arange(piece_rows, dtype=jnp.int32)
    source_stripe = gathered_rows // query_total
    within = gathered_rows % query_total
    key_place = (
        within // tokens_here * stripe_count + source_stripe
    ) * tokens_here + within % tokens_here
    maxima, totals, running = attend(
        carried,
        queries,
        query_place,
        query_turn,
        pieces[0],
        pieces[1],
        key_place,
        jnp.take(turn_ids, key_place),
        jnp.take(judged, key_place),
        scaling,
    )
    result = (
        (running / totals[:, :, None])
        .astype(jnp.bfloat16)
        .reshape(query_total, 1, heads_here * HEAD_DIM)
    )
    returned = lax.all_to_all(result, "ulysses", split_axis=0, concat_axis=1, tiled=True)
    return returned.reshape(tokens_here, ulysses_count * heads_here * HEAD_DIM)


def solution(mesh):
    placed = (
        P(("groups", "ulysses", "seq"), None),
        P(("groups", "ulysses", "seq"), None),
        P(("groups", "ulysses", "seq"), None),
        P("groups"),
        P("groups"),
    )
    return jax.shard_map(
        shards,
        mesh=mesh,
        in_specs=placed,
        out_specs=P(("groups", "ulysses", "seq"), None),
        check_vma=False,
    )
```

profile of v0, /device:TPU:0, one launch (start us, length us, event | category | flops | bytes accessed | tf_op | source)
XLA Modules:
  0.0 126.2 jit_solution(8405274671733121284)
XLA Ops:
  0.0 0.9 copy-done
  0.9 0.7 copy_bitcast_fusion.2
  1.6 7.3 %all-to-all-start = ((bf16[64,8,128]{2,0,1:T(8,128)(2,1)}), bf16[64,8,128]{2,0,1:T(8,128)(2,1)S(1)}, u32[]{:S(2)}, u32[]{:S(2)}) async-start(bf16[64,8,128]{2,0,1:T(8,128)(2,1)} %copy_bitcast_fusion.2), calls=%async_computation | async-start | bytes 262144 | tf_op jit(solution)/shard_map/all_to_all | solution.py:147
  8.9 1.6 %copy_bitcast_fusion.1 = bf16[64,8,128]{2,0,1:T(8,128)(2,1)} fusion(bf16[64,1024]{1,0:T(8,128)(2,1)} %param.11), kind=kLoop, calls=%fused_computation.40 | loop fusion | bytes 262144 | tf_op jit(solution)/shard_map/reshape;reshape | solution.py:114
  10.4 5.8 %all-to-all-done = bf16[64,8,128]{2,0,1:T(8,128)(2,1)S(1)} async-done(((bf16[64,8,128]{2,0,1:T(8,128)(2,1)}), bf16[64,8,128]{2,0,1:T(8,128)(2,1)S(1)}, u32[]{:S(2)}, u32[]{:S(2)}) %all-to-all-start) | async-done | bytes 131104 | tf_op jit(solution)/shard_map/all_to_all | solution.py:147
  16.2 3.4 %all-to-all-start.2 = ((bf16[64,8,128]{2,0,1:T(8,128)(2,1)}), bf16[64,8,128]{2,0,1:T(8,128)(2,1)S(1)}, u32[]{:S(2)}, u32[]{:S(2)}) async-start(bf16[64,8,128]{2,0,1:T(8,128)(2,1)} %copy_bitcast_fusion.1), calls=%async_computation.2 | async-start | bytes 262144 | tf_op jit(solution)/shard_map/all_to_all | solution.py:150
  19.6 2.3 %copy.51 = bf16[8,8,8,1024]{3,2,0,1:T(8,128)(2,1)} copy(bf16[8,8,8,1024]{3,2,1,0:T(8,128)(2,1)} %bitcast.71) | data formatting | bytes 2097152 | tf_op jit(solution)/shard_map/reshape | solution.py:128
  21.9 5.0 %all-to-all-done.2 = bf16[64,8,128]{2,0,1:T(8,128)(2,1)S(1)} async-done(((bf16[64,8,128]{2,0,1:T(8,128)(2,1)}), bf16[64,8,128]{2,0,1:T(8,128)(2,1)S(1)}, u32[]{:S(2)}, u32[]{:S(2)}) %all-to-all-start.2) | async-done | bytes 131104 | tf_op jit(solution)/shard_map/all_to_all | solution.py:150
  26.9 3.6 %all-to-all-start.1 = ((bf16[64,8,1024]{2,0,1:T(8,128)(2,1)}), bf16[64,8,1024]{2,0,1:T(8,128)(2,1)S(1)}, u32[]{:S(2)}, u32[]{:S(2)}) async-start(bf16[64,8,1024]{2,0,1:T(8,128)(2,1)} %bitcast.66), calls=%async_computation.1 | async-start | bytes 2097152 | tf_op jit(solution)/shard_map/all_to_all | solution.py:127
  30.5 5.7 %gather_fusion = s32[1024]{0:T(1024)S(1)} fusion(s32[1024]{0:T(1024)} %param.12, s32[1024]{0:T(1024)S(1)} %broadcast_clamp_fusion), kind=kCustom, calls=%fused_computation | custom fusion | bytes 12288 | tf_op jit(solution)/shard_map/jit(_take)/gather | solution.py:175
  36.3 2.3 %gather_fusion.1 = s32[512]{0:T(512)S(1)} fusion(s32[1024]{0:T(1024)S(1)} %copy-done.1, s32[1024]{0:T(1024)S(1)} %pad_clamp_fusion), kind=kCustom, calls=%fused_computation.1 | custom fusion | bytes 6144 | tf_op jit(solution)/shard_map/jit(_take)/gather | solution.py:140
  38.6 0.2 fusion.24
  38.8 6.8 %gather_fusion.2 = pred[1024]{0:T(1024)(128)(4,1)S(1)} fusion(pred[1024]{0:T(1024)(128)(4,1)S(1)} %fusion.24, s32[1024]{0:T(1024)S(1)} %broadcast_clamp_fusion), kind=kCustom, calls=%fused_computation.2 | custom fusion | bytes 6144 | tf_op jit(solution)/shard_map/jit(_take)/gather | solution.py:176
  45.6 0.6 broadcast_select_fusion.1
  46.2 1.3 %and_select_fusion.6 = (s32[512]{0:T(512)}, s32[]{:T(128)}) fusion(s32[512]{0:T(512)S(1)} %gather_fusion.1, s32[]{:T(128)} %axis_index.12), kind=kLoop, calls=%fused_computation.115 | loop fusion | flops 12287 | bytes 4104 | tf_op jit(solution)/shard_map/jit(_take)/select_n | solution.py:140
  47.5 0.6 fusion.35
  48.1 2.0 %all_gather.6 = bf16[1024,128]{1,0:T(8,128)(2,1)S(1)} all-gather(bf16[512,128]{1,0:T(8,128)(2,1)S(1)} %bitcast.72), channel_id=1, replica_groups=mesh['groups'=2,'ulysses'=8,'seq'=2] {'seq'}, dimensions={0}, use_global_device_ids=true | all-gather | bytes 393216 | tf_op jit(solution)/shard_map/all_gather | solution.py:157
  50.1 2.1 %all_gather.7 = bf16[1024,128]{1,0:T(8,128)(2,1)} all-gather(bf16[512,128]{1,0:T(8,128)(2,1)S(1)} %bitcast.73), channel_id=1, replica_groups=mesh['groups'=2,'ulysses'=8,'seq'=2] {'seq'}, dimensions={0}, use_global_device_ids=true | all-gather | bytes 393216 | tf_op jit(solution)/shard_map/all_gather | solution.py:158
  52.2 1.9 %all-to-all-done.1 = bf16[64,8,1024]{2,0,1:T(8,128)(2,1)S(1)} async-done(((bf16[64,8,1024]{2,0,1:T(8,128)(2,1)}), bf16[64,8,1024]{2,0,1:T(8,128)(2,1)S(1)}, u32[]{:S(2)}, u32[]{:S(2)}) %all-to-all-start.1) | async-done | bytes 1048608 | tf_op jit(solution)/shard_map/all_to_all | solution.py:127
  54.0 0.3 copy.45
  54.3 0.1 copy.36
  54.5 0.6 dynamic_slice.75
  55.1 0.1 dynamic_slice.76
  55.2 31.6 %while.31 = (s32[]{:T(128)}, f32[512,8]{0,1:T(8,128)S(1)}, f32[512,8]{0,1:T(8,128)}, f32[512,8,128]{2,0,1:T(8,128)S(1)}, s32[1024]{0:T(1024)}, /*index=5*/s32[]{...) while((s32[]{:T(128)}, f32[512,8]{0,1:T(8,128)S(1)}, ...), condition=%wide.region_8.9_spmd.clone, body=%wide.region_2.8_spmd.clone.sunk | while | flops 1098925056 | bytes 33209420 | solution.py:96
  55.2 2.0 %fusion.67 = (s32[]{:T(128)}, s32[512]{0:T(512)}) fusion(s32[1024]{0:T(1024)} %get-tuple-element.768, s32[]{:T(128)} %select_n.391), kind=kLoop, calls=%fused_computation.117.clone.1 | loop fusion | flops 511 | bytes 4104 | tf_op jit(solution)/shard_map/while/body/eval_jaxpr/while/body/eval_jaxpr/reduce_min | solution.py:79
  58.6 0.6 iota.233
  59.2 0.6 iota_shift-right-logical_fusion.6
  59.8 0.5 broadcast_compare_fusion.2
  60.3 0.6 rem.490
  60.9 0.6 ne.390
  61.5 9.5 %conditional.3 = ((f32[512,8]{0,1:T(8,128)S(1)}, f32[512,8]{0,1:T(8,128)}, f32[512,8,128]{2,0,1:T(8,128)S(1)})) conditional(s32[]{:T(128)} %convert_element_type.25, (f32[512,8]{0,1:T(8,128)S(1)}, f32[512,8]{0,1:T(8,128)}, f32[512,8,128]{2,0,1:T(8,128)S(1)}) %tuple.76, (s32[512]{0:T(512)}, s32[512]{0:T(512)}, s32[1024]{0:T(1024)}, s32[]{:T(128)}, ...), branch_computations={%region_4.4_spmd, %region_5.7_spmd.clone} | conditional | flops 1098922496 | bytes 33194124 | solution.py:78
  61.5 0.8 fusion.18
  62.3 0.8 dynamic_slice.78
  63.0 0.7 dynamic_slice.79
  63.7 1.0 or_and_fusion
  64.8 0.0 copy-start.2
  64.8 1.5 %fusion.4 = (f32[512,8]{0,1:T(8,128)S(1)}, f32[512,512,8]{1,0,2:T(8,128)S(1)}) fusion(pred[512,512]{0,1:T(8,128)(4,1)S(1)} %or_and_fusion, bf16[512,8,128]{2,0,1:T(8,128)(2,1)S(1)} %get-tuple-element.552, bf16[1024,128]{1,0:T(8,128)(2,1)S(1)} %get-tuple-element.551, s32[]{:T(128)} %get-tuple-element.548), kind=kOutput, calls=%fused_computation.8 | convolution fusion | flops 543158272 | bytes 9846788 | tf_op jit(solution)/shard_map/while/body/eval_jaxpr/while/body/eval_jaxpr/cond/branch_1_fun/qhd,kd->qhk/dot_general | solution.py:25
  66.3 1.7 %fusion.3 = f32[512,8]{0,1:T(8,128)S(1)} fusion(f32[512,512,8]{1,0,2:T(8,128)S(1)} %get-tuple-element.622, f32[512,8]{0,1:T(8,128)S(1)} %max.5, pred[512,512]{0,1:T(8,128)(4,1)S(1)} %or_and_fusion), kind=kLoop, calls=%fused_computation.7 | loop fusion | flops 8384512 | bytes 8683520 | tf_op jit(solution)/shard_map/while/body/eval_jaxpr/while/body/eval_jaxpr/cond/branch_1_fun/reduce_sum | solution.py:35
  68.1 0.0 copy-start.3
  68.1 2.8 %multiply_add_fusion = f32[512,8,128]{2,0,1:T(8,128)S(1)} fusion(f32[512,8,128]{2,0,1:T(8,128)S(1)} %get-tuple-element.554, f32[512,512,8]{1,0,2:T(8,128)S(1)} %get-tuple-element.622, f32[512,8]{0,1:T(8,128)S(1)} %max.5, pred[512,512]{0,1:T(8,128)(4,1)S(1)} %or_and_fusion, f32[512,8]{0,1:T(8,128)S(1)} %get-tuple-element.618, ...), kind=kOutput, calls=%fused_computation.11 | convolution fusion | flops 546308096 | bytes 13008900 | tf_op jit(solution)/shard_map/while/body/eval_jaxpr/while/body/eval_jaxpr/cond/branch_1_fun/qhk,kd->qhd/dot_general | solution.py:36
  71.0 2.0 %fusion.67 = (s32[]{:T(128)}, s32[512]{0:T(512)}) fusion(s32[1024]{0:T(1024)} %get-tuple-element.768, s32[]{:T(128)} %select_n.391), kind=kLoop, calls=%fused_computation.117.clone.1 | loop fusion | flops 511 | bytes 4104 | tf_op jit(solution)/shard_map/while/body/eval_jaxpr/while/body/eval_jaxpr/reduce_min | solution.py:79
  74.4 0.6 iota.233
  74.9 0.6 iota_shift-right-logical_fusion.6
  75.5 0.5 broadcast_compare_fusion.2
  76.1 0.6 rem.490
  76.7 0.6 ne.390
  77.3 9.5 %conditional.3 = ((f32[512,8]{0,1:T(8,128)S(1)}, f32[512,8]{0,1:T(8,128)}, f32[512,8,128]{2,0,1:T(8,128)S(1)})) conditional(s32[]{:T(128)} %convert_element_type.25, (f32[512,8]{0,1:T(8,128)S(1)}, f32[512,8]{0,1:T(8,128)}, f32[512,8,128]{2,0,1:T(8,128)S(1)}) %tuple.76, (s32[512]{0:T(512)}, s32[512]{0:T(512)}, s32[1024]{0:T(1024)}, s32[]{:T(128)}, ...), branch_computations={%region_4.4_spmd, %region_5.7_spmd.clone} | conditional | flops 1098922496 | bytes 33194124 | solution.py:78
  77.3 0.8 fusion.18
  78.1 0.8 dynamic_slice.78
  78.8 0.7 dynamic_slice.79
  79.5 1.0 or_and_fusion
  80.6 1.5 %fusion.4 = (f32[512,8]{0,1:T(8,128)S(1)}, f32[512,512,8]{1,0,2:T(8,128)S(1)}) fusion(pred[512,512]{0,1:T(8,128)(4,1)S(1)} %or_and_fusion, bf16[512,8,128]{2,0,1:T(8,128)(2,1)S(1)} %get-tuple-element.552, bf16[1024,128]{1,0:T(8,128)(2,1)S(1)} %get-tuple-element.551, s32[]{:T(128)} %get-tuple-element.548), kind=kOutput, calls=%fused_computation.8 | convolution fusion | flops 543158272 | bytes 9846788 | tf_op jit(solution)/shard_map/while/body/eval_jaxpr/while/body/eval_jaxpr/cond/branch_1_fun/qhd,kd->qhk/dot_general | solution.py:25
  82.1 1.7 %fusion.3 = f32[512,8]{0,1:T(8,128)S(1)} fusion(f32[512,512,8]{1,0,2:T(8,128)S(1)} %get-tuple-element.622, f32[512,8]{0,1:T(8,128)S(1)} %max.5, pred[512,512]{0,1:T(8,128)(4,1)S(1)} %or_and_fusion), kind=kLoop, calls=%fused_computation.7 | loop fusion | flops 8384512 | bytes 8683520 | tf_op jit(solution)/shard_map/while/body/eval_jaxpr/while/body/eval_jaxpr/cond/branch_1_fun/reduce_sum | solution.py:35
  83.9 2.8 %multiply_add_fusion = f32[512,8,128]{2,0,1:T(8,128)S(1)} fusion(f32[512,8,128]{2,0,1:T(8,128)S(1)} %get-tuple-element.554, f32[512,512,8]{1,0,2:T(8,128)S(1)} %get-tuple-element.622, f32[512,8]{0,1:T(8,128)S(1)} %max.5, pred[512,512]{0,1:T(8,128)(4,1)S(1)} %or_and_fusion, f32[512,8]{0,1:T(8,128)S(1)} %get-tuple-element.618, ...), kind=kOutput, calls=%fused_computation.11 | convolution fusion | flops 546308096 | bytes 13008900 | tf_op jit(solution)/shard_map/while/body/eval_jaxpr/while/body/eval_jaxpr/cond/branch_1_fun/qhk,kd->qhd/dot_general | solution.py:36
  86.8 1.9 %copy.37 = f32[512,8,128]{0,2,1:T(8,128)} copy(f32[512,8,128]{2,0,1:T(8,128)S(1)} %get-tuple-element.428) | data formatting | bytes 4194304 | tf_op jit(solution)/shard_map/while/body/eval_jaxpr/while | solution.py:96
  88.7 1.9 %divide_convert_fusion = bf16[512,8,128]{0,2,1:T(8,128)(2,1)S(1)} fusion(f32[512,8,128]{0,2,1:T(8,128)} %copy.37, f32[512,8]{0,1:T(8,128)} %get-tuple-element.429), kind=kLoop, calls=%fused_computation.36 | loop fusion | flops 1048576 | bytes 3162112 | tf_op jit(solution)/shard_map/convert_element_type | solution.py:181
  90.5 0.5 broadcast.462
  91.0 1.5 %reduce = bf16[512,1024]{0,1:T(8,128)(2,1)S(1)} reduce(bf16[512,1,1024]{0,2,1:T(8,128)(2,1)S(1)} %bitcast.67, bf16[]{:T(256)} %broadcast.462), dimensions={1}, to_apply=%copy.38.reduce_sub_computation | reduce | bytes 2097154 | tf_op jit(solution)/shard_map/reshape | solution.py:182
  92.5 0.5 copy.52
  93.0 0.8 reshape.331
  93.8 29.9 %all_to_all.60 = bf16[8,2,32768]{2,1,0:T(2,128)(2,1)S(1)} all-to-all(bf16[8,2,32768]{2,1,0:T(2,128)(2,1)S(1)} %reshape.331), channel_id=1, replica_groups=mesh['groups'=2,'ulysses'=8,'seq'=2] {'ulysses'}, dimensions={0} | all-to-all | bytes 2097152 | tf_op jit(solution)/shard_map/all_to_all | solution.py:184
  123.7 1.0 reshape.332
  124.8 0.4 copy.41
  125.2 1.1 copy.46
  (26 shorter events, 0.1 us)
Async XLA Ops:
  0.0 0.9 copy-start
  0.0 36.2 %copy-start.1 = (s32[1024]{0:T(1024)S(1)}, s32[1024]{0:T(1024)}, u32[]{:S(2)}) copy-start(s32[1024]{0:T(1024)} %param.12) | copy-start | bytes 12292
  0.9 37.7 %copy-start.5 = (s32[128]{0:T(128)S(1)}, s32[128]{0:T(128)}, u32[]{:S(2)}) copy-start(s32[128]{0:T(128)} %param.13) | copy-start | bytes 1540
  1.6 14.6 %all-to-all-start = ((bf16[64,8,128]{2,0,1:T(8,128)(2,1)}), bf16[64,8,128]{2,0,1:T(8,128)(2,1)S(1)}, u32[]{:S(2)}, u32[]{:S(2)}) async-start(bf16[64,8,128]{2,0,1:T(8,128)(2,1)} %copy_bitcast_fusion.2), calls=%async_computation | async-start | bytes 262144 | tf_op jit(solution)/shard_map/all_to_all | solution.py:147
  16.2 10.7 %all-to-all-start.2 = ((bf16[64,8,128]{2,0,1:T(8,128)(2,1)}), bf16[64,8,128]{2,0,1:T(8,128)(2,1)S(1)}, u32[]{:S(2)}, u32[]{:S(2)}) async-start(bf16[64,8,128]{2,0,1:T(8,128)(2,1)} %copy_bitcast_fusion.1), calls=%async_computation.2 | async-start | bytes 262144 | tf_op jit(solution)/shard_map/all_to_all | solution.py:150
  26.9 27.2 %all-to-all-start.1 = ((bf16[64,8,1024]{2,0,1:T(8,128)(2,1)}), bf16[64,8,1024]{2,0,1:T(8,128)(2,1)S(1)}, u32[]{:S(2)}, u32[]{:S(2)}) async-start(bf16[64,8,1024]{2,0,1:T(8,128)(2,1)} %bitcast.66), calls=%async_computation.1 | async-start | bytes 2097152 | tf_op jit(solution)/shard_map/all_to_all | solution.py:127
  64.8 3.3 %copy-start.2 = (f32[512,8]{0,1:T(8,128)S(1)}, f32[512,8]{0,1:T(8,128)}, u32[]{:S(2)}) copy-start(f32[512,8]{0,1:T(8,128)} %get-tuple-element.553) | copy-start | bytes 49156 | tf_op jit(solution)/shard_map/while/body/eval_jaxpr/while/body/eval_jaxpr/cond
  64.8 3.3 %copy-start.4 = (bf16[1024,128]{1,0:T(8,128)(2,1)S(1)}, bf16[1024,128]{1,0:T(8,128)(2,1)}, u32[]{:S(2)}) copy-start(bf16[1024,128]{1,0:T(8,128)(2,1)} %get-tuple-element.555) | copy-start | bytes 786436 | tf_op jit(solution)/shard_map/while/body/eval_jaxpr/while/body/eval_jaxpr/cond
  68.1 2.9 %copy-start.3 = (f32[512,8]{0,1:T(8,128)}, f32[512,8]{0,1:T(8,128)S(1)}, u32[]{:S(2)}) copy-start(f32[512,8]{0,1:T(8,128)S(1)} %get-tuple-element.726) | copy-start | bytes 49156 | tf_op jit(solution)/shard_map/while/body/eval_jaxpr/while/body/eval_jaxpr/cond
  80.6 3.3 %copy-start.2 = (f32[512,8]{0,1:T(8,128)S(1)}, f32[512,8]{0,1:T(8,128)}, u32[]{:S(2)}) copy-start(f32[512,8]{0,1:T(8,128)} %get-tuple-element.553) | copy-start | bytes 49156 | tf_op jit(solution)/shard_map/while/body/eval_jaxpr/while/body/eval_jaxpr/cond
  80.6 3.3 %copy-start.4 = (bf16[1024,128]{1,0:T(8,128)(2,1)S(1)}, bf16[1024,128]{1,0:T(8,128)(2,1)}, u32[]{:S(2)}) copy-start(bf16[1024,128]{1,0:T(8,128)(2,1)} %get-tuple-element.555) | copy-start | bytes 786436 | tf_op jit(solution)/shard_map/while/body/eval_jaxpr/while/body/eval_jaxpr/cond
  83.9 2.9 %copy-start.3 = (f32[512,8]{0,1:T(8,128)}, f32[512,8]{0,1:T(8,128)S(1)}, u32[]{:S(2)}) copy-start(f32[512,8]{0,1:T(8,128)S(1)} %get-tuple-element.726) | copy-start | bytes 49156 | tf_op jit(solution)/shard_map/while/body/eval_jaxpr/while/body/eval_jaxpr/cond
where the time goes:
time: 127 us; the launch traced here: 126 us
  local copies, waits for them, and re-layouts  34.1 us (27%)
  blocking collectives  34 us (27%)
  other arithmetic  19.5 us (15%)
  starting transfers between devices  14.2 us (11%)
  waiting for transfers between devices  12.6 us (10%)
  matrix products  8.7 us (7%)
  loops' own time  2.94 us (2%)
    all_to_all x1, blocking collectives, shards(): lax.all_to_all(result, 'ulysses', split_axis=0, concat_axis=1, tiled=True)  29.9 us
    all_to_all x1, starting transfers between devices, shards(): lax.all_to_all(spread(key_states, ulysses_count), 'ulysses', split_axis=1...  7.28 us
    gather x1, local copies, waits for them, and re-layouts, shards(): jnp.take(judged, key_place)  6.8 us
    all_to_all x1, waiting for transfers between devices, shards(): lax.all_to_all(spread(key_states, ulysses_count), 'ulysses', split_axis=1...  5.76 us
    gather x1, local copies, waits for them, and re-layouts, shards(): jnp.take(turn_ids, key_place)  5.72 us
    dot_general x2, matrix products, absorb(): jnp.einsum('qhk,kd->qhd', weights.astype(jnp.bfloat16), values_block, pre...  5.69 us
    unnamed x13, local copies, waits for them, and re-layouts  5.12 us
    all_to_all x1, waiting for transfers between devices, shards(): lax.all_to_all(spread(value_states, ulysses_count), 'ulysses', split_axis...  4.99 us
  transfers between devices with their start and end apart: 3, of which 3 were waited for; matrix products, arithmetic and copies ran while one was open for 17% of the time, Pallas kernels for 0%

commit v1 on v0

--- a/solution.py
+++ b/solution.py
@@ -143,10 +143,17 @@
         jnp.zeros((query_total, heads_here), jnp.float32),
         jnp.zeros((query_total, heads_here, HEAD_DIM), jnp.float32),
     )
+
+    def mix_slices(local, along_axis):
+        return jnp.concatenate(
+            lax.all_to_all(
+                jnp.stack(jnp.split(local, lax.axis_size(along_axis), axis=1)), along_axis, 0, 0
+            ),
+            axis=0,
+        )
+
     keys_out, values_out = (
-        lax.all_to_all(
-            spread(key_states, ulysses_count), "ulysses", split_axis=1, concat_axis=0, tiled=True
-        ),
+        mix_slices(spread(key_states, ulysses_count), "ulysses"),
         lax.all_to_all(
             spread(value_states, ulysses_count), "ulysses", split_axis=1, concat_axis=0, tiled=True
         ),

time: 127 us -> 130 us (1.024)
  local copies, waits for them, and re-layouts: 34.1 us -> 36.5 us
  waiting for transfers between devices: 12.6 us -> 14.8 us
    unnamed x13 -> x21, local copies, waits for them, and re-layouts: 5.12 us -> 9.44 us
    another operation x2 -> x1, local copies, waits for them, and re-layouts: 2.26 us -> 0.67 us  [spread(): return widened.reshape(row_count, copies, HEAD_DIM)]
  transfers between devices with their start and end apart: 3 -> 3, of which waited for: 3 -> 3; matrix products, arithmetic and copies ran while one was open for 17% -> 15% of each run, Pallas kernels for 0% -> 0%
where the time goes in v1:
time: 130 us; the launch traced here: 129 us
  local copies, waits for them, and re-layouts  36.5 us (28%)
  blocking collectives  32.8 us (25%)
  other arithmetic  19.2 us (15%)
  waiting for transfers between devices  14.8 us (11%)
  starting transfers between devices  14.2 us (11%)
  matrix products  8.7 us (7%)
  loops' own time  2.63 us (2%)
    all_to_all x1, blocking collectives, shards(): lax.all_to_all(result, 'ulysses', split_axis=0, concat_axis=1, tiled=True)  28.7 us
    unnamed x21, local copies, waits for them, and re-layouts  9.44 us
    all_to_all x1, starting transfers between devices, mix_slices(): lax.all_to_all(jnp.stack(jnp.split(local, lax.axis_size(along_axis), axis...  7.29 us
    gather x1, local copies, waits for them, and re-layouts, shards(): jnp.take(judged, key_place)  6.8 us
    all_to_all x1, waiting for transfers between devices, mix_slices(): lax.all_to_all(jnp.stack(jnp.split(local, lax.axis_size(along_axis), axis...  6.67 us
    dot_general x2, matrix products, absorb(): jnp.einsum('qhk,kd->qhd', weights.astype(jnp.bfloat16), values_block, pre...  5.68 us
    all_to_all x1, waiting for transfers between devices, shards(): lax.all_to_all(spread(value_states, ulysses_count), 'ulysses', split_axis...  4.99 us
    gather x1, local copies, waits for them, and re-layouts, shards(): jnp.take(turn_ids, key_place)  4.53 us
  transfers between devices with their start and end apart: 3, of which 3 were waited for; matrix products, arithmetic and copies ran while one was open for 15% of the time, Pallas kernels for 0%

profile of v1, /device:TPU:0, one launch (start us, length us, event | category | flops | bytes accessed | tf_op | source)
XLA Modules:
  0.0 129.1 jit_solution(7194257376772716173)
XLA Ops:
  0.0 1.0 copy.162
  1.2 0.6 constant_dynamic-update-slice_fusion.7
  1.8 0.6 constant_dynamic-update-slice_fusion.6
  2.4 0.6 constant_dynamic-update-slice_fusion.5
  3.0 0.6 constant_dynamic-update-slice_fusion.4
  3.6 0.6 constant_dynamic-update-slice_fusion.3
  4.3 0.6 constant_dynamic-update-slice_fusion.2
  4.9 0.6 constant_dynamic-update-slice_fusion.1
  5.5 0.6 constant_dynamic-update-slice_fusion
  6.1 7.3 %all-to-all-start = ((bf16[8,64,1,128]{3,1,2,0:T(8,128)(2,1)}), bf16[8,64,1,128]{3,1,2,0:T(8,128)(2,1)S(1)}, u32[]{:S(2)}, u32[]{:S(2)}) async-start(bf16[8,64,1,128]{3,1,2,0:T(8,128)(2,1)} %constant_dynamic-update-slice_fusion), calls=%async_computation | async-start | bytes 262144 | tf_op jit(solution)/shard_map/all_to_all | solution.py:149
  13.4 0.7 copy_bitcast_fusion.1
  14.0 6.7 %all-to-all-done = bf16[8,64,1,128]{3,1,2,0:T(8,128)(2,1)S(1)} async-done(((bf16[8,64,1,128]{3,1,2,0:T(8,128)(2,1)}), bf16[8,64,1,128]{3,1,2,0:T(8,128)(2,1)S(1)}, u32[]{:S(2)}, u32[]{:S(2)}) %all-to-all-start) | async-done | bytes 131104 | tf_op jit(solution)/shard_map/all_to_all | solution.py:149
  20.7 3.4 %all-to-all-start.2 = ((bf16[64,8,128]{2,0,1:T(8,128)(2,1)}), bf16[64,8,128]{2,0,1:T(8,128)(2,1)S(1)}, u32[]{:S(2)}, u32[]{:S(2)}) async-start(bf16[64,8,128]{2,0,1:T(8,128)(2,1)} %copy_bitcast_fusion.1), calls=%async_computation.2 | async-start | bytes 262144 | tf_op jit(solution)/shard_map/all_to_all | solution.py:157
  24.1 2.3 %copy.176 = bf16[8,8,8,1024]{3,2,0,1:T(8,128)(2,1)} copy(bf16[8,8,8,1024]{3,2,1,0:T(8,128)(2,1)} %bitcast.81) | data formatting | bytes 2097152 | tf_op jit(solution)/shard_map/reshape | solution.py:128
  26.4 5.0 %all-to-all-done.2 = bf16[64,8,128]{2,0,1:T(8,128)(2,1)S(1)} async-done(((bf16[64,8,128]{2,0,1:T(8,128)(2,1)}), bf16[64,8,128]{2,0,1:T(8,128)(2,1)S(1)}, u32[]{:S(2)}, u32[]{:S(2)}) %all-to-all-start.2) | async-done | bytes 131104 | tf_op jit(solution)/shard_map/all_to_all | solution.py:157
  31.4 3.6 %all-to-all-start.1 = ((bf16[64,8,1024]{2,0,1:T(8,128)(2,1)}), bf16[64,8,1024]{2,0,1:T(8,128)(2,1)S(1)}, u32[]{:S(2)}, u32[]{:S(2)}) async-start(bf16[64,8,1024]{2,0,1:T(8,128)(2,1)} %bitcast.75), calls=%async_computation.1 | async-start | bytes 2097152 | tf_op jit(solution)/shard_map/all_to_all | solution.py:127
  35.0 4.5 %gather_fusion = s32[1024]{0:T(1024)S(1)} fusion(s32[1024]{0:T(1024)S(1)} %copy-done.1, s32[1024]{0:T(1024)S(1)} %broadcast_clamp_fusion), kind=kCustom, calls=%fused_computation | custom fusion | bytes 12288 | tf_op jit(solution)/shard_map/jit(_take)/gather | solution.py:182
  39.6 2.3 %gather_fusion.1 = s32[512]{0:T(512)S(1)} fusion(s32[1024]{0:T(1024)S(1)} %copy-done.1, s32[1024]{0:T(1024)S(1)} %pad_clamp_fusion), kind=kCustom, calls=%fused_computation.1 | custom fusion | bytes 6144 | tf_op jit(solution)/shard_map/jit(_take)/gather | solution.py:140
  42.1 6.8 %gather_fusion.2 = pred[1024]{0:T(1024)(128)(4,1)S(1)} fusion(pred[1024]{0:T(1024)(128)(4,1)S(1)} %fusion.24, s32[1024]{0:T(1024)S(1)} %broadcast_clamp_fusion), kind=kCustom, calls=%fused_computation.2 | custom fusion | bytes 6144 | tf_op jit(solution)/shard_map/jit(_take)/gather | solution.py:183
  48.9 0.6 broadcast_select_fusion.1
  49.5 1.2 and_select_fusion.6
  50.7 0.6 fusion.35
  51.3 2.0 %all_gather.6 = bf16[1024,128]{1,0:T(8,128)(2,1)S(1)} all-gather(bf16[512,128]{1,0:T(8,128)(2,1)S(1)} %bitcast.82), channel_id=1, replica_groups=mesh['groups'=2,'ulysses'=8,'seq'=2] {'seq'}, dimensions={0}, use_global_device_ids=true | all-gather | bytes 393216 | tf_op jit(solution)/shard_map/all_gather | solution.py:164
  53.3 2.1 %all_gather.7 = bf16[1024,128]{1,0:T(8,128)(2,1)} all-gather(bf16[512,128]{1,0:T(8,128)(2,1)S(1)} %bitcast.83), channel_id=1, replica_groups=mesh['groups'=2,'ulysses'=8,'seq'=2] {'seq'}, dimensions={0}, use_global_device_ids=true | all-gather | bytes 393216 | tf_op jit(solution)/shard_map/all_gather | solution.py:165
  55.4 3.2 %all-to-all-done.1 = bf16[64,8,1024]{2,0,1:T(8,128)(2,1)S(1)} async-done(((bf16[64,8,1024]{2,0,1:T(8,128)(2,1)}), bf16[64,8,1024]{2,0,1:T(8,128)(2,1)S(1)}, u32[]{:S(2)}, u32[]{:S(2)}) %all-to-all-start.1) | async-done | bytes 1048608 | tf_op jit(solution)/shard_map/all_to_all | solution.py:127
  59.0 0.6 dynamic_slice.75
  59.7 31.1 %while.31 = (s32[]{:T(128)}, f32[512,8]{0,1:T(8,128)S(1)}, f32[512,8]{0,1:T(8,128)}, f32[512,8,128]{2,0,1:T(8,128)S(1)}, s32[1024]{0:T(1024)}, /*index=5*/s32[]{...) while((s32[]{:T(128)}, f32[512,8]{0,1:T(8,128)S(1)}, ...), condition=%wide.region_8.9_spmd.clone, body=%wide.region_2.8_spmd.clone.sunk | while | flops 1098925056 | bytes 33209420 | solution.py:96
  59.7 2.0 %fusion.67 = (s32[]{:T(128)}, s32[512]{0:T(512)}) fusion(s32[1024]{0:T(1024)} %get-tuple-element.893, s32[]{:T(128)} %select_n.391), kind=kLoop, calls=%fused_computation.124.clone.1 | loop fusion | flops 511 | bytes 4104 | tf_op jit(solution)/shard_map/while/body/eval_jaxpr/while/body/eval_jaxpr/reduce_min | solution.py:79
  62.9 0.6 iota.233
  63.5 0.6 iota_shift-right-logical_fusion.6
  64.1 0.5 broadcast_compare_fusion.2
  64.6 0.6 rem.490
  65.2 0.6 ne.390
  65.7 9.5 %conditional.3 = ((f32[512,8]{0,1:T(8,128)S(1)}, f32[512,8]{0,1:T(8,128)}, f32[512,8,128]{2,0,1:T(8,128)S(1)})) conditional(s32[]{:T(128)} %convert_element_type.25, (f32[512,8]{0,1:T(8,128)S(1)}, f32[512,8]{0,1:T(8,128)}, f32[512,8,128]{2,0,1:T(8,128)S(1)}) %tuple.92, (s32[512]{0:T(512)}, s32[512]{0:T(512)}, s32[1024]{0:T(1024)}, s32[]{:T(128)}, ...), branch_computations={%region_4.4_spmd, %region_5.7_spmd.clone} | conditional | flops 1098922496 | bytes 33194124 | solution.py:78
  65.7 0.8 fusion.18
  66.5 0.8 dynamic_slice.78
  67.3 0.7 dynamic_slice.79
  68.0 1.0 or_and_fusion
  69.1 1.5 %fusion.4 = (f32[512,8]{0,1:T(8,128)S(1)}, f32[512,512,8]{1,0,2:T(8,128)S(1)}) fusion(pred[512,512]{0,1:T(8,128)(4,1)S(1)} %or_and_fusion, bf16[512,8,128]{2,0,1:T(8,128)(2,1)S(1)} %get-tuple-element.669, bf16[1024,128]{1,0:T(8,128)(2,1)S(1)} %get-tuple-element.668, s32[]{:T(128)} %get-tuple-element.665), kind=kOutput, calls=%fused_computation.8 | convolution fusion | flops 543158272 | bytes 9846788 | tf_op jit(solution)/shard_map/while/body/eval_jaxpr/while/body/eval_jaxpr/cond/branch_1_fun/qhd,kd->qhk/dot_general | solution.py:25
  70.6 1.7 %fusion.3 = f32[512,8]{0,1:T(8,128)S(1)} fusion(f32[512,512,8]{1,0,2:T(8,128)S(1)} %get-tuple-element.739, f32[512,8]{0,1:T(8,128)S(1)} %max.5, pred[512,512]{0,1:T(8,128)(4,1)S(1)} %or_and_fusion), kind=kLoop, calls=%fused_computation.7 | loop fusion | flops 8384512 | bytes 8683520 | tf_op jit(solution)/shard_map/while/body/eval_jaxpr/while/body/eval_jaxpr/cond/branch_1_fun/reduce_sum | solution.py:35
  72.4 2.8 %multiply_add_fusion = f32[512,8,128]{2,0,1:T(8,128)S(1)} fusion(f32[512,8,128]{2,0,1:T(8,128)S(1)} %get-tuple-element.671, f32[512,512,8]{1,0,2:T(8,128)S(1)} %get-tuple-element.739, f32[512,8]{0,1:T(8,128)S(1)} %max.5, pred[512,512]{0,1:T(8,128)(4,1)S(1)} %or_and_fusion, f32[512,8]{0,1:T(8,128)S(1)} %get-tuple-element.735, ...), kind=kOutput, calls=%fused_computation.11 | convolution fusion | flops 546308096 | bytes 13008900 | tf_op jit(solution)/shard_map/while/body/eval_jaxpr/while/body/eval_jaxpr/cond/branch_1_fun/qhk,kd->qhd/dot_general | solution.py:36
  75.3 2.0 %fusion.67 = (s32[]{:T(128)}, s32[512]{0:T(512)}) fusion(s32[1024]{0:T(1024)} %get-tuple-element.893, s32[]{:T(128)} %select_n.391), kind=kLoop, calls=%fused_computation.124.clone.1 | loop fusion | flops 511 | bytes 4104 | tf_op jit(solution)/shard_map/while/body/eval_jaxpr/while/body/eval_jaxpr/reduce_min | solution.py:79
  78.4 0.6 iota.233
  79.0 0.6 iota_shift-right-logical_fusion.6
  79.6 0.5 broadcast_compare_fusion.2
  80.1 0.6 rem.490
  80.7 0.6 ne.390
  81.3 9.5 %conditional.3 = ((f32[512,8]{0,1:T(8,128)S(1)}, f32[512,8]{0,1:T(8,128)}, f32[512,8,128]{2,0,1:T(8,128)S(1)})) conditional(s32[]{:T(128)} %convert_element_type.25, (f32[512,8]{0,1:T(8,128)S(1)}, f32[512,8]{0,1:T(8,128)}, f32[512,8,128]{2,0,1:T(8,128)S(1)}) %tuple.92, (s32[512]{0:T(512)}, s32[512]{0:T(512)}, s32[1024]{0:T(1024)}, s32[]{:T(128)}, ...), branch_computations={%region_4.4_spmd, %region_5.7_spmd.clone} | conditional | flops 1098922496 | bytes 33194124 | solution.py:78
  81.3 0.8 fusion.18
  82.1 0.8 dynamic_slice.78
  82.9 0.7 dynamic_slice.79
  83.6 1.0 or_and_fusion
  84.6 1.5 %fusion.4 = (f32[512,8]{0,1:T(8,128)S(1)}, f32[512,512,8]{1,0,2:T(8,128)S(1)}) fusion(pred[512,512]{0,1:T(8,128)(4,1)S(1)} %or_and_fusion, bf16[512,8,128]{2,0,1:T(8,128)(2,1)S(1)} %get-tuple-element.669, bf16[1024,128]{1,0:T(8,128)(2,1)S(1)} %get-tuple-element.668, s32[]{:T(128)} %get-tuple-element.665), kind=kOutput, calls=%fused_computation.8 | convolution fusion | flops 543158272 | bytes 9846788 | tf_op jit(solution)/shard_map/while/body/eval_jaxpr/while/body/eval_jaxpr/cond/branch_1_fun/qhd,kd->qhk/dot_general | solution.py:25
  86.1 1.7 %fusion.3 = f32[512,8]{0,1:T(8,128)S(1)} fusion(f32[512,512,8]{1,0,2:T(8,128)S(1)} %get-tuple-element.739, f32[512,8]{0,1:T(8,128)S(1)} %max.5, pred[512,512]{0,1:T(8,128)(4,1)S(1)} %or_and_fusion), kind=kLoop, calls=%fused_computation.7 | loop fusion | flops 8384512 | bytes 8683520 | tf_op jit(solution)/shard_map/while/body/eval_jaxpr/while/body/eval_jaxpr/cond/branch_1_fun/reduce_sum | solution.py:35
  87.9 2.8 %multiply_add_fusion = f32[512,8,128]{2,0,1:T(8,128)S(1)} fusion(f32[512,8,128]{2,0,1:T(8,128)S(1)} %get-tuple-element.671, f32[512,512,8]{1,0,2:T(8,128)S(1)} %get-tuple-element.739, f32[512,8]{0,1:T(8,128)S(1)} %max.5, pred[512,512]{0,1:T(8,128)(4,1)S(1)} %or_and_fusion, f32[512,8]{0,1:T(8,128)S(1)} %get-tuple-element.735, ...), kind=kOutput, calls=%fused_computation.11 | convolution fusion | flops 546308096 | bytes 13008900 | tf_op jit(solution)/shard_map/while/body/eval_jaxpr/while/body/eval_jaxpr/cond/branch_1_fun/qhk,kd->qhd/dot_general | solution.py:36
  90.8 1.9 %copy.147 = f32[512,8,128]{0,2,1:T(8,128)} copy(f32[512,8,128]{2,0,1:T(8,128)S(1)} %get-tuple-element.428) | data formatting | bytes 4194304 | tf_op jit(solution)/shard_map/while/body/eval_jaxpr/while | solution.py:96
  92.7 1.9 %divide_convert_fusion = bf16[512,8,128]{0,2,1:T(8,128)(2,1)S(1)} fusion(f32[512,8,128]{0,2,1:T(8,128)} %copy.147, f32[512,8]{0,1:T(8,128)} %get-tuple-element.429), kind=kLoop, calls=%fused_computation.36 | loop fusion | flops 1048576 | bytes 3162112 | tf_op jit(solution)/shard_map/convert_element_type | solution.py:188
  94.6 0.5 broadcast.462
  95.1 1.5 %reduce = bf16[512,1024]{0,1:T(8,128)(2,1)S(1)} reduce(bf16[512,1,1024]{0,2,1:T(8,128)(2,1)S(1)} %bitcast.76, bf16[]{:T(256)} %broadcast.462), dimensions={1}, to_apply=%copy.148.reduce_sub_computation | reduce | bytes 2097154 | tf_op jit(solution)/shard_map/reshape | solution.py:189
  96.5 0.5 copy.177
  97.1 0.8 reshape.326
  97.9 28.7 %all_to_all.50 = bf16[8,2,32768]{2,1,0:T(2,128)(2,1)S(1)} all-to-all(bf16[8,2,32768]{2,1,0:T(2,128)(2,1)S(1)} %reshape.326), channel_id=1, replica_groups=mesh['groups'=2,'ulysses'=8,'seq'=2] {'ulysses'}, dimensions={0} | all-to-all | bytes 2097152 | tf_op jit(solution)/shard_map/all_to_all | solution.py:191
  126.6 1.0 reshape.327
  128.0 1.1 copy.164
  (35 shorter events, 1.5 us)
Async XLA Ops:
  0.0 13.4 %copy-start = (bf16[64,1024]{1,0:T(8,128)(2,1)S(1)}, bf16[64,1024]{1,0:T(8,128)(2,1)}, u32[]{:S(2)}) copy-start(bf16[64,1024]{1,0:T(8,128)(2,1)} %param.11) | copy-start | bytes 393220
  0.0 35.0 %copy-start.1 = (s32[1024]{0:T(1024)S(1)}, s32[1024]{0:T(1024)}, u32[]{:S(2)}) copy-start(s32[1024]{0:T(1024)} %param.12) | copy-start | bytes 12292
  0.0 41.9 %copy-start.5 = (s32[128]{0:T(128)S(1)}, s32[128]{0:T(128)}, u32[]{:S(2)}) copy-start(s32[128]{0:T(128)} %param.13) | copy-start | bytes 1540
  6.1 14.6 %all-to-all-start = ((bf16[8,64,1,128]{3,1,2,0:T(8,128)(2,1)}), bf16[8,64,1,128]{3,1,2,0:T(8,128)(2,1)S(1)}, u32[]{:S(2)}, u32[]{:S(2)}) async-start(bf16[8,64,1,128]{3,1,2,0:T(8,128)(2,1)} %constant_dynamic-update-slice_fusion), calls=%async_computation | async-start | bytes 262144 | tf_op jit(solution)/shard_map/all_to_all | solution.py:149
  20.7 10.7 %all-to-all-start.2 = ((bf16[64,8,128]{2,0,1:T(8,128)(2,1)}), bf16[64,8,128]{2,0,1:T(8,128)(2,1)S(1)}, u32[]{:S(2)}, u32[]{:S(2)}) async-start(bf16[64,8,128]{2,0,1:T(8,128)(2,1)} %copy_bitcast_fusion.1), calls=%async_computation.2 | async-start | bytes 262144 | tf_op jit(solution)/shard_map/all_to_all | solution.py:157
  31.4 27.2 %all-to-all-start.1 = ((bf16[64,8,1024]{2,0,1:T(8,128)(2,1)}), bf16[64,8,1024]{2,0,1:T(8,128)(2,1)S(1)}, u32[]{:S(2)}, u32[]{:S(2)}) async-start(bf16[64,8,1024]{2,0,1:T(8,128)(2,1)} %bitcast.75), calls=%async_computation.1 | async-start | bytes 2097152 | tf_op jit(solution)/shard_map/all_to_all | solution.py:127
  69.0 3.3 %copy-start.2 = (f32[512,8]{0,1:T(8,128)S(1)}, f32[512,8]{0,1:T(8,128)}, u32[]{:S(2)}) copy-start(f32[512,8]{0,1:T(8,128)} %get-tuple-element.670) | copy-start | bytes 49156 | tf_op jit(solution)/shard_map/while/body/eval_jaxpr/while/body/eval_jaxpr/cond
  69.0 3.3 %copy-start.4 = (bf16[1024,128]{1,0:T(8,128)(2,1)S(1)}, bf16[1024,128]{1,0:T(8,128)(2,1)}, u32[]{:S(2)}) copy-start(bf16[1024,128]{1,0:T(8,128)(2,1)} %get-tuple-element.672) | copy-start | bytes 786436 | tf_op jit(solution)/shard_map/while/body/eval_jaxpr/while/body/eval_jaxpr/cond
  72.4 2.9 %copy-start.3 = (f32[512,8]{0,1:T(8,128)}, f32[512,8]{0,1:T(8,128)S(1)}, u32[]{:S(2)}) copy-start(f32[512,8]{0,1:T(8,128)S(1)} %get-tuple-element.851) | copy-start | bytes 49156 | tf_op jit(solution)/shard_map/while/body/eval_jaxpr/while/body/eval_jaxpr/cond
  84.6 3.3 %copy-start.2 = (f32[512,8]{0,1:T(8,128)S(1)}, f32[512,8]{0,1:T(8,128)}, u32[]{:S(2)}) copy-start(f32[512,8]{0,1:T(8,128)} %get-tuple-element.670) | copy-start | bytes 49156 | tf_op jit(solution)/shard_map/while/body/eval_jaxpr/while/body/eval_jaxpr/cond
  84.6 3.3 %copy-start.4 = (bf16[1024,128]{1,0:T(8,128)(2,1)S(1)}, bf16[1024,128]{1,0:T(8,128)(2,1)}, u32[]{:S(2)}) copy-start(bf16[1024,128]{1,0:T(8,128)(2,1)} %get-tuple-element.672) | copy-start | bytes 786436 | tf_op jit(solution)/shard_map/while/body/eval_jaxpr/while/body/eval_jaxpr/cond
  87.9 2.9 %copy-start.3 = (f32[512,8]{0,1:T(8,128)}, f32[512,8]{0,1:T(8,128)S(1)}, u32[]{:S(2)}) copy-start(f32[512,8]{0,1:T(8,128)S(1)} %get-tuple-element.851) | copy-start | bytes 49156 | tf_op jit(solution)/shard_map/while/body/eval_jaxpr/while/body/eval_jaxpr/cond
